TPU v7x, 32 devices: a whole 2x2x4 slice. The times are simulated.
32 devices in a mesh: dp: 8 (over z, x), psr: 4 (over y, core).
Axes of the slice: x: 2, y: 2, z: 4, core: 2. Of those that a mesh axis runs over, the one named last changes fastest.
Arguments:
- basis: bfloat16 [32, 4, 8, 128, 256], P(('dp', 'psr')), may hold values from -6 to 6
- residual: bfloat16 [32, 4, 8, 128], P(('dp', 'psr')), may hold values from -6 to 6
- sigma: bfloat16 [32, 4, 8, 128], P(('dp', 'psr')), may hold values from 0.5 to 2
- counts: int32 [32, 4, 8], P(('dp', 'psr')), may hold values from 0 to 128
- pulsar: int32 [32, 4, 8], P(('dp', 'psr')), may hold values from 0 to 3
- ecorr: float32 [16], replicated, may hold values from 0.2 to 2
Outputs:
- gram: float32 [16, 256, 256], P('psr', 'dp')
- rhs: float32 [16, 256], P('psr', 'dp')
- totals: float32 [2], replicated
All inputs are finite; a program needn't handle non-finite values.
Results may differ from a plain program's by a relative error of at most 0.0055.
Values may be sent and summed in bfloat16 or wider, within the bound.
A program may use at most 64 MiB of HBM per device.

v0:
```python
import jax
import jax.numpy as jnp
from jax import lax
from jax.sharding import PartitionSpec as P

PG = 4


def slot_terms(basis, residual, sigma, counts, pulsar, group_ids, ecorr):
    sig = sigma.astype(jnp.float32)
    res = residual.astype(jnp.float32)
    rowpos = lax.broadcasted_iota(jnp.int32, sig.shape, 2)
    valid = rowpos < counts[..., None]
    inverse = jnp.where(valid, 1.0 / (sig * sig), jnp.float32(0.0))
    weighted = (inverse[..., None] * basis).astype(jnp.bfloat16)
    global_id = group_ids[:, None] * PG + pulsar
    table = jnp.arange(ecorr.shape[0], dtype=jnp.int32)
    chosen = jnp.sum(jnp.where(global_id[..., None] == table, ecorr, jnp.float32(0.0)), axis=-1)
    jitter = chosen * chosen
    total = jnp.sum(inverse, axis=2)
    coef = jitter / (1.0 + jitter * total)
    column = jnp.sum(weighted.astype(jnp.float32), axis=2)
    project = jnp.sum(weighted.astype(jnp.float32) * res[..., None], axis=2)
    wsum = jnp.sum(inverse * res, axis=2)
    chi = jnp.sum(inverse * res * res) - jnp.sum(coef * wsum * wsum)
    logdet = jnp.sum(jnp.where(valid, jnp.log(sig * sig), jnp.float32(0.0))) + jnp.sum(
        jnp.log(1.0 + jitter * total)
    )
    adjusted = project - (coef * wsum)[..., None] * column
    grams = []
    sums = []
    for member in range(PG):
        picked = pulsar == member
        masked = jnp.where(picked[..., None, None], weighted, jnp.zeros((), jnp.bfloat16))
        first = jnp.einsum("gslk,gslm->gkm", basis, masked, preferred_element_type=jnp.float32)
        scale = jnp.where(picked, coef, jnp.float32(0.0))
        minus = jnp.einsum(
            "gs,gsk,gsm->gkm", scale, column, column, precision=lax.Precision.HIGHEST
        )
        grams.append(first - minus)
        sums.append(jnp.sum(jnp.where(picked[..., None], adjusted, jnp.float32(0.0)), axis=1))
    return (jnp.stack(grams, axis=1), jnp.stack(sums, axis=1), logdet, chi)


def on_device(basis, residual, sigma, counts, pulsar, ecorr):
    groups = lax.axis_size("psr")
    ndp = lax.axis_size("dp")
    width = basis.shape[-1]
    rows = basis.shape[-2]
    slots = basis.shape[2]
    share = width // ndp
    group_ids = jnp.arange(groups, dtype=jnp.int32)
    gram, rhs, logdet, chi = slot_terms(
        basis[0], residual[0], sigma[0], counts[0], pulsar[0], group_ids, ecorr
    )
    gram_rows = (
        gram.reshape(groups, PG, ndp, share, width)
        .transpose(2, 0, 1, 3, 4)
        .reshape(ndp * groups * PG * share, width)
    )
    rhs_rows = (
        rhs.reshape(groups, PG, ndp, share).transpose(2, 0, 1, 3).reshape(ndp * groups * PG * share)
    )
    gram_part, rhs_part = (
        lax.psum_scatter(gram_rows, ("dp", "psr"), scatter_dimension=0, tiled=True),
        lax.psum_scatter(rhs_rows, ("dp", "psr"), scatter_dimension=0, tiled=True),
    )
    gram_part = gram_part.reshape(PG, share, width)
    rhs_part = rhs_part.reshape(PG, share)
    summed = lax.psum((logdet, chi), ("dp", "psr"))
    norm_rows = float(ndp * slots * rows)
    all_rows = float(ndp * groups * groups * slots * rows)
    totals = jnp.stack([summed[0], summed[1]]) / all_rows
    return (gram_part / norm_rows, rhs_part / norm_rows, totals)


def solution(mesh):
    return jax.shard_map(
        on_device,
        mesh=mesh,
        in_specs=(
            P(("dp", "psr"), None, None, None, None),
            P(("dp", "psr"), None, None, None),
            P(("dp", "psr"), None, None, None),
            P(("dp", "psr"), None, None),
            P(("dp", "psr"), None, None),
            P(),
        ),
        out_specs=(P("psr", "dp", None), P("psr", "dp"), P()),
        check_vma=False,
    )
```

profile of v0, /device:TPU:0, one launch (start us, length us, event | category | flops | bytes accessed | tf_op | source)
XLA Modules:
  0.0 185.6 jit_solution(12531503588392629328)
XLA Ops:
  7.2 0.0 copy-start
  7.2 0.0 reduce-scatter.2.cloned.1.call-start
  7.2 0.8 bitcast_convert_fusion
  8.1 0.8 bitcast_add_fusion
  8.8 0.8 select_reduce_fusion.4
  9.6 1.5 fusion.45
  11.1 0.6 multiply_reduce_fusion.2
  11.8 0.7 broadcast_select_fusion.3
  12.5 2.8 %fusion = (f32[4,8,256]{2,1,0:T(8,128)S(1)}, f32[4,8,256]{2,1,0:T(8,128)S(1)}) fusion(f32[4,8,128]{2,1,0:T(8,128)S(1)} %bitcast_convert_fusion, bf16[1,4,8,128,256]{4,3,2,1,0:T(8,128)(2,1)} %param.6, f32[4,8,128]{2,1,0:T(8,128)S(1)} %get-tuple-element.29), kind=kLoop, calls=%fused_computation.2 | loop fusion | flops 7323648 | bytes 2195456 | tf_op jit(solution)/shard_map/reduce_sum | solution.py:23
  15.3 2.3 %fusion.22 = f32[4,256,256]{2,1,0:T(8,128)S(1)} fusion(bf16[1,4,8,128,256]{4,3,2,1,0:T(8,128)(2,1)S(1)} %copy-done, f32[4,8,128]{2,1,0:T(8,128)S(1)} %get-tuple-element.29, pred[4,8]{1,0:T(4,128)(4,1)S(1)} %get-tuple-element.36), kind=kOutput, calls=%fused_computation.22 | convolution fusion | flops 541065216 | bytes 3162144 | tf_op jit(solution)/shard_map/gslk,gslm->gkm/dot_general | solution.py:35
  17.6 2.3 %fusion.27 = f32[4,256,256]{2,1,0:T(8,128)S(1)} fusion(bf16[1,4,8,128,256]{4,3,2,1,0:T(8,128)(2,1)S(1)} %copy-done, f32[4,8,128]{2,1,0:T(8,128)S(1)} %get-tuple-element.29, pred[4,8]{1,0:T(4,128)(4,1)S(1)} %get-tuple-element.34), kind=kOutput, calls=%fused_computation.23 | convolution fusion | flops 541065216 | bytes 3162144 | tf_op jit(solution)/shard_map/gslk,gslm->gkm/dot_general | solution.py:35
  19.8 2.3 %fusion.32 = f32[4,256,256]{2,1,0:T(8,128)S(1)} fusion(bf16[1,4,8,128,256]{4,3,2,1,0:T(8,128)(2,1)S(1)} %copy-done, f32[4,8,128]{2,1,0:T(8,128)S(1)} %get-tuple-element.29, pred[4,8]{1,0:T(4,128)(4,1)S(1)} %get-tuple-element.32), kind=kOutput, calls=%fused_computation.24 | convolution fusion | flops 541065216 | bytes 3162144 | tf_op jit(solution)/shard_map/gslk,gslm->gkm/dot_general | solution.py:35
  22.1 2.3 %fusion.17 = f32[4,256,256]{2,1,0:T(8,128)S(1)} fusion(bf16[1,4,8,128,256]{4,3,2,1,0:T(8,128)(2,1)S(1)} %copy-done, f32[4,8,128]{2,1,0:T(8,128)S(1)} %get-tuple-element.29, pred[4,8]{1,0:T(4,128)(4,1)S(1)} %get-tuple-element.22), kind=kOutput, calls=%fused_computation.21 | convolution fusion | flops 541065216 | bytes 3162144 | tf_op jit(solution)/shard_map/gslk,gslm->gkm/dot_general | solution.py:35
  24.4 1.1 convolution_subtract_fusion.2
  25.5 1.1 convolution_subtract_fusion.1
  26.6 1.1 convolution_subtract_fusion
  27.7 1.1 convolution_subtract_fusion.3
  28.8 0.6 pad_maximum_fusion
  29.4 2.3 %copy.56 = f32[4,4,8,32,256]{4,3,1,0,2:T(8,128)} copy(f32[4,4,8,32,256]{4,3,2,0,1:T(8,128)S(1)} %pad_maximum_fusion) | data formatting | bytes 8388608 | tf_op jit(solution)/shard_map/stack | solution.py:42
  31.7 0.0 reduce-scatter.2.cloned.1.call-update
  31.7 0.1 select_reduce_fusion.3
  31.8 0.1 stack.44
  31.9 0.1 stack.47
  32.0 0.1 stack.46
  32.1 0.1 stack.45
  32.2 0.1 reshape.137
  34.9 44.1 %all-reduce.1 = (f32[4096]{0:T(1024)S(1)}, f32[1]{0:T(128)}, f32[1]{0:T(128)}) all-reduce(f32[4096]{0:T(1024)S(1)} %reshape.137, f32[1]{0:T(128)} %bitcast.28, f32[1]{0:T(128)} %bitcast.27), channel_id=3, replica_groups=mesh['dp'=8,'psr'=4] {'dp','psr'}, use_global_device_ids=true, to_apply=%region_10.11.clone | all-reduce | flops 4098 | bytes 32784
  79.0 0.1 dynamic-slice_multiply_fusion
  79.1 0.7 div.48
  79.7 1.8 maximum_multiply_fusion
  81.6 95.7 %reduce-scatter.2.cloned.1.call-done = f32[128,256]{1,0:T(8,128)} async-done(((f32[4096,256]{1,0:T(8,128)}), f32[128,256]{1,0:T(8,128)}) %reduce-scatter.2.cloned.1.call-update) | async-done | bytes 131088 | tf_op jit(solution)/shard_map/reduce_scatter | solution.py:65
  177.2 1.6 broadcast_multiply_fusion
  (4 shorter events, 0.1 us)
Async XLA Ops:
  7.2 8.1 %copy-start = (bf16[1,4,8,128,256]{4,3,2,1,0:T(8,128)(2,1)S(1)}, bf16[1,4,8,128,256]{4,3,2,1,0:T(8,128)(2,1)}, u32[]{:S(2)}) copy-start(bf16[1,4,8,128,256]{4,3,2,1,0:T(8,128)(2,1)} %param.6) | copy-start | bytes 6291460
  7.2 170.0 %reduce-scatter.2.cloned.1.call-start = ((), (), s32[]{:S(2)}) async-start(), calls=%async_computation.1 | async-start | bytes 4325376 | tf_op jit(solution)/shard_map/reduce_scatter | solution.py:65
Sparse Core Ops, SparseCore 0:
  31.8 145.3 reduce-scatter.1
where the time goes:
time: 186 us
  waiting for transfers between devices  95.7 us (51%)
  blocking collectives  44.1 us (24%)
  between operations  16.7 us (9%)
  matrix products  13.5 us (7%)
  other arithmetic  12.3 us (7%)
  local copies, waits for them, and re-layouts  3.37 us (2%)
    reduce_scatter x1, waiting for transfers between devices, on_device(): lax.psum_scatter(gram_rows, ('dp', 'psr'), scatter_dimension=0, tiled=True)  95.7 us
    unnamed x1, blocking collectives  44.1 us
    dot_general x4, matrix products, slot_terms(): jnp.einsum('gslk,gslm->gkm', basis, masked, preferred_element_type=jnp.fl...  9.01 us
    dot_general x4, matrix products, slot_terms(): jnp.einsum('gs,gsk,gsm->gkm', scale, column, column, precision=lax.Precis...  4.45 us
  transfers between devices with their start and end apart: 1, of which 1 were waited for; matrix products, arithmetic and copies ran while one was open for 2% of the time, Pallas kernels for 0%

commit v1 on v0

--- a/solution.py
+++ b/solution.py
@@ -1,9 +1,327 @@
+import functools
+
 import jax
 import jax.numpy as jnp
 from jax import lax
+from jax.experimental import pallas as pl
+from jax.experimental.pallas import tpu as pltpu
 from jax.sharding import PartitionSpec as P
 
 PG = 4
+MESH = pl.DeviceIdType.MESH
+F32 = jnp.float32
+BF16 = jnp.bfloat16
+
+
+def column_of(row):
+    n = row.shape[1]
+    eye = lax.broadcasted_iota(jnp.int32, (n, n), 0) == lax.broadcasted_iota(jnp.int32, (n, n), 1)
+    return jnp.sum(jnp.where(eye, jnp.broadcast_to(row, (n, n)), F32(0.0)), axis=1, keepdims=True)
+
+
+def group_terms(g, basis, res_ref, sig_ref, cnt_ref, pul_ref, ecorr_ref):
+    slots, rows, width = basis.shape
+    sig = sig_ref[g].astype(F32)
+    res = res_ref[g].astype(F32)
+    counts = column_of(cnt_ref[pl.ds(g, 1), :].astype(F32))
+    pulsar = column_of(pul_ref[pl.ds(g, 1), :].astype(F32))
+    lane = lax.broadcasted_iota(jnp.int32, (slots, rows), 1)
+    valid = lane.astype(F32) < counts
+    var = sig * sig
+    inverse = jnp.where(valid, 1.0 / var, F32(0.0))
+    total = jnp.sum(inverse, axis=1, keepdims=True)
+    n_table = ecorr_ref.shape[1]
+    table = lax.broadcasted_iota(jnp.int32, (slots, n_table), 1).astype(F32)
+    ids = pulsar + (g * PG).astype(F32)
+    chosen = jnp.sum(
+        jnp.where(ids == table, jnp.broadcast_to(ecorr_ref[...], (slots, n_table)), F32(0.0)),
+        axis=1,
+        keepdims=True,
+    )
+    jitter = chosen * chosen
+    coef = jitter / (1.0 + jitter * total)
+    wsum = jnp.sum(inverse * res, axis=1, keepdims=True)
+    first = lane == 0
+    chi = inverse * res * res - jnp.where(first, coef * wsum * wsum, F32(0.0))
+    logdet = jnp.where(valid, jnp.log(var), F32(0.0)) + jnp.where(
+        first, jnp.log(1.0 + jitter * total), F32(0.0)
+    )
+    tot = jnp.concatenate(
+        [jnp.sum(logdet, axis=0, keepdims=True), jnp.sum(chi, axis=0, keepdims=True)], axis=1
+    )
+
+    inv_t = inverse.T
+    adj_t = (coef * inverse).T
+    blocks = [basis[s] for s in range(slots)]
+    weighted = [
+        (inv_t[:, s : s + 1] * blocks[s].astype(F32)).astype(BF16) for s in range(slots)
+    ]
+    member = lax.broadcasted_iota(jnp.int32, (PG, rows), 0).astype(F32)
+    onehot = jnp.concatenate(
+        [
+            jnp.where(member == jnp.broadcast_to(pulsar[s : s + 1], (PG, rows)), F32(1.0), F32(0.0))
+            for s in range(slots)
+        ],
+        axis=1,
+    )
+    slot = lax.broadcasted_iota(jnp.int32, (slots, rows), 0)
+    marks = jnp.concatenate(
+        [jnp.where(slot == s, F32(1.0), F32(0.0)) for s in range(slots)], axis=1
+    )
+    res_row = jnp.concatenate([res[s : s + 1] for s in range(slots)], axis=1)
+    left = jnp.concatenate([marks, onehot * res_row, onehot], axis=0).astype(BF16)
+    sums = jnp.dot(left, jnp.concatenate(weighted, axis=0), preferred_element_type=F32)
+    column = sums[:slots]
+    project = sums[slots : slots + PG]
+    cw = coef * wsum
+    minus = jnp.concatenate(
+        [
+            jnp.sum(jnp.where(pulsar == F32(m), cw, F32(0.0)) * column, axis=0, keepdims=True)
+            for m in range(PG)
+        ],
+        axis=0,
+    )
+    rhs = project - minus
+    adjusted = jnp.concatenate(
+        [
+            (weighted[s].astype(F32) - adj_t[:, s : s + 1] * column[s : s + 1]).astype(BF16)
+            for s in range(slots)
+        ],
+        axis=0,
+    )
+    turned = jnp.concatenate([b.T for b in blocks], axis=1)
+    pick = onehot.astype(BF16)
+
+    def gram(m):
+        return jnp.dot(turned * pick[m : m + 1], adjusted, preferred_element_type=F32)
+
+    return gram, rhs, tot
+
+
+def kernel(
+    ndp, norm_rows, all_rows,
+    basis_ref, res_ref, sig_ref, cnt_ref, pul_ref, ecorr_ref,
+    gram_ref, rhs_ref, tot_ref,
+    bbuf, out0, in0, out1, in1, own_a, own_b, send_a, send_b,
+    in_y, in_xa, in_xb, out_x, in_x, out_y, in_y2, part, out_z, in_z,
+    s_core, r_core, s_y, r_y, s_x, r_x, s_z, r_z,
+    load_sem, send_sem, recv_sem, zsend_sem, zrecv_sem,
+):
+    nz = ndp // 2
+    half = PG // 2
+    dp = lax.axis_index("dp")
+    psr = lax.axis_index("psr")
+    c, y = psr % 2, psr // 2
+    x, z = dp % 2, dp // 2
+    c2, y2, x2 = 1 - c, 1 - y, 1 - x
+    core_peer = (dp, y * 2 + c2)
+    y_peer = (dp, y2 * 2 + c)
+    x_peer = (z * 2 + x2, psr)
+    order = (y2 * 2 + c2, y2 * 2 + c, y * 2 + c2, psr)
+
+    loads = []
+    for i, g in enumerate(order):
+        load = pltpu.make_async_copy(basis_ref.at[g], bbuf.at[i], load_sem.at[i])
+        load.start()
+        loads.append(load)
+
+    z_peers = [(((z + k) % nz) * 2 + x, psr) for k in range(1, nz)]
+    barrier = pltpu.get_barrier_semaphore()
+    for peer in [core_peer, y_peer, x_peer] + z_peers:
+        pl.semaphore_signal(barrier, inc=1, device_id=peer, device_id_type=MESH)
+
+    def send(i, src, dst, peer):
+        copy = pltpu.make_async_remote_copy(
+            src_ref=src, dst_ref=dst, send_sem=send_sem.at[i], recv_sem=recv_sem.at[i],
+            device_id=peer, device_id_type=MESH,
+        )
+        copy.start()
+        return copy
+
+    def shaped(v, ref):
+        return v.reshape(ref.shape[1:])
+
+    def terms(i):
+        loads[i].wait()
+        return group_terms(order[i], bbuf.at[i], res_ref, sig_ref, cnt_ref, pul_ref, ecorr_ref)
+
+    gram, rhs0, tot = terms(0)
+    for m in range(PG):
+        out0[m] = shaped(gram(m).astype(BF16), out0)
+    pl.semaphore_wait(barrier, 2 + nz)
+    c0 = send(0, out0, in0, core_peer)
+
+    gram, rhs1, t = terms(1)
+    tot = tot + t
+    for m in range(PG):
+        own_a[m] = shaped(gram(m), own_a)
+
+    gram, rhs2, t = terms(2)
+    tot = tot + t
+    for m in range(PG):
+        out1[m] = shaped(gram(m).astype(BF16), out1)
+    c1 = send(1, out1, in1, core_peer)
+
+    c0.wait_recv()
+    send_a[...] = (own_a[...] + in0[...].astype(F32)).astype(BF16)
+    cy = send(2, send_a.at[pl.ds(0, half)], in_y, y_peer)
+    cxa = send(3, send_a.at[pl.ds(half, PG - half), :, x2], in_xa, x_peer)
+
+    gram, rhs3, t = terms(3)
+    tot = tot + t
+    for m in range(PG):
+        own_b[m] = shaped(gram(m), own_b)
+
+    pad = jnp.zeros((3, tot.shape[1]), F32)
+    s_core[...] = jnp.concatenate([rhs0, rhs2, tot, pad, jnp.zeros((4, tot.shape[1]), F32)], axis=0)
+    cs0 = send(4, s_core, r_core, core_peer)
+
+    c1.wait_recv()
+    own_b[...] = own_b[...] + in1[...].astype(F32)
+    send_b[...] = own_b[pl.ds(half, PG - half), :, x2].astype(BF16)
+    cxb = send(5, send_b, in_xb, x_peer)
+
+    cs0.wait_recv()
+    rhs1 = rhs1 + r_core[0:PG]
+    rhs3 = rhs3 + r_core[PG : 2 * PG]
+    tot = tot + r_core[2 * PG : 2 * PG + 1]
+    s_y[...] = jnp.concatenate([rhs1, tot, pad], axis=0)
+    cs1 = send(6, s_y, r_y, y_peer)
+
+    cxa.wait_recv()
+    out_y[...] = (
+        send_a[pl.ds(half, PG - half), :, x].astype(F32) + in_xa[...].astype(F32)
+    ).astype(BF16)
+    cy2 = send(7, out_y, in_y2, y_peer)
+
+    cy.wait_recv()
+    out_x[...] = (own_b[pl.ds(0, half), :, x2] + in_y[:, :, x2].astype(F32)).astype(BF16)
+    cx1 = send(8, out_x, in_x, x_peer)
+    part[0:half] = own_b[pl.ds(0, half), :, x] + in_y[:, :, x].astype(F32)
+
+    cs1.wait_recv()
+    rhs3 = rhs3 + r_y[0:PG]
+    tot = tot + r_y[PG : PG + 1]
+    s_x[...] = jnp.concatenate([rhs3, tot, pad], axis=0)
+    cs2 = send(9, s_x, r_x, x_peer)
+
+    def z_send(h, k, src, dst):
+        n = h * (nz - 1) + k - 1
+        copy = pltpu.make_async_remote_copy(
+            src_ref=src, dst_ref=dst, send_sem=zsend_sem.at[n], recv_sem=zrecv_sem.at[n],
+            device_id=z_peers[k - 1], device_id_type=MESH,
+        )
+        copy.start()
+        return copy
+
+    z_copies = []
+
+    def z_stage(h):
+        piece = pl.ds(h * half, half)
+        for k in range(1, nz):
+            zt = (z + k) % nz
+            out_z[piece, k - 1] = part[piece, zt].astype(BF16)
+            z_copies.append(z_send(h, k, out_z.at[piece, k - 1], in_z.at[piece, k - 1]))
+
+    cxb.wait_recv()
+    cy2.wait_recv()
+    part[half:PG] = (
+        own_b[pl.ds(half, PG - half), :, x] + in_xb[...].astype(F32) + in_y2[...].astype(F32)
+    )
+    z_stage(1)
+    cx1.wait_recv()
+    part[0:half] = part[0:half] + in_x[...].astype(F32)
+    z_stage(0)
+
+    cs2.wait_recv()
+    rhs3 = rhs3 + r_x[0:PG]
+    tot = tot + r_x[PG : PG + 1]
+    s_z[...] = jnp.concatenate([rhs3, tot, pad], axis=0)
+    small = [z_send(2, k, s_z, r_z.at[k - 1]) for k in range(1, nz)]
+
+    for h in (1, 0):
+        piece = pl.ds(h * half, half)
+        acc = part[piece, z]
+        for k in range(1, nz):
+            z_copies[(1 - h) * (nz - 1) + k - 1].wait_recv()
+            acc = acc + in_z[piece, k - 1].astype(F32)
+        gram_ref[piece] = acc / norm_rows
+
+    for k in range(1, nz):
+        small[k - 1].wait_recv()
+        rhs3 = rhs3 + r_z[k - 1, 0:PG]
+        tot = tot + r_z[k - 1, PG : PG + 1]
+    share = rhs_ref.shape[1]
+    mine = jnp.zeros((PG, share), F32)
+    for e in range(ndp):
+        mine = mine + jnp.where(dp == e, rhs3[:, e * share : (e + 1) * share], F32(0.0))
+    rhs_ref[...] = mine / norm_rows
+    rows = tot.shape[1] // 2
+    tot_ref[0] = jnp.sum(tot[:, :rows]) / all_rows
+    tot_ref[1] = jnp.sum(tot[:, rows:]) / all_rows
+
+    for copy in [c0, c1, cy, cxa, cs0, cxb, cs1, cy2, cx1, cs2] + z_copies + small:
+        copy.wait_send()
+
+
+def fused(basis, residual, sigma, counts, pulsar, ecorr):
+    ndp = lax.axis_size("dp")
+    groups, slots, rows, width = basis.shape[1:]
+    share = width // ndp
+    nz = ndp // 2
+    half = PG // 2
+    norm_rows = float(ndp * slots * rows)
+    all_rows = float(ndp * groups * groups * slots * rows)
+    vmem = pl.BlockSpec(memory_space=pltpu.VMEM)
+    full = (PG, nz, 2, share, width)
+    hfull = (half, nz, 2, share, width)
+    hpar = (half, nz, share, width)
+    n_z = 3 * (nz - 1)
+    return pl.pallas_call(
+        functools.partial(kernel, ndp, norm_rows, all_rows),
+        out_shape=(
+            jax.ShapeDtypeStruct((PG, share, width), F32),
+            jax.ShapeDtypeStruct((PG, share), F32),
+            jax.ShapeDtypeStruct((2,), F32),
+        ),
+        in_specs=[pl.BlockSpec(memory_space=pl.ANY)] + [vmem] * 5,
+        out_specs=(vmem, vmem, pl.BlockSpec(memory_space=pltpu.SMEM)),
+        scratch_shapes=[
+            pltpu.VMEM((groups, slots, rows, width), BF16),
+            pltpu.VMEM(full, BF16),
+            pltpu.VMEM(full, BF16),
+            pltpu.VMEM(full, BF16),
+            pltpu.VMEM(full, BF16),
+            pltpu.VMEM(full, F32),
+            pltpu.VMEM(full, F32),
+            pltpu.VMEM(full, BF16),
+            pltpu.VMEM(hpar, BF16),
+            pltpu.VMEM(hfull, BF16),
+            pltpu.VMEM(hpar, BF16),
+            pltpu.VMEM(hpar, BF16),
+            pltpu.VMEM(hpar, BF16),
+            pltpu.VMEM(hpar, BF16),
+            pltpu.VMEM(hpar, BF16),
+            pltpu.VMEM(hpar, BF16),
+            pltpu.VMEM((PG, nz, share, width), F32),
+            pltpu.VMEM((PG, nz - 1, share, width), BF16),
+            pltpu.VMEM((PG, nz - 1, share, width), BF16),
+            pltpu.VMEM((4 * PG, width), F32),
+            pltpu.VMEM((4 * PG, width), F32),
+            pltpu.VMEM((2 * PG, width), F32),
+            pltpu.VMEM((2 * PG, width), F32),
+            pltpu.VMEM((2 * PG, width), F32),
+            pltpu.VMEM((2 * PG, width), F32),
+            pltpu.VMEM((2 * PG, width), F32),
+            pltpu.VMEM((nz - 1, 2 * PG, width), F32),
+            pltpu.SemaphoreType.DMA((groups,)),
+            pltpu.SemaphoreType.DMA((10,)),
+            pltpu.SemaphoreType.DMA((10,)),
+            pltpu.SemaphoreType.DMA((n_z,)),
+            pltpu.SemaphoreType.DMA((n_z,)),
+        ],
+        compiler_params=pltpu.CompilerParams(collective_id=0, has_side_effects=True),
+    )(basis[0], residual[0], sigma[0], counts[0], pulsar[0], ecorr.reshape(1, -1))
 
 
 def slot_terms(basis, residual, sigma, counts, pulsar, group_ids, ecorr):
@@ -75,8 +393,16 @@
 
 
 def solution(mesh):
+    def step(basis, *rest):
+        groups, _, rows, width = basis.shape[1:]
+        ndp = lax.axis_size("dp")
+        tiled = ndp % 2 == 0 and ndp > 2 and width % (16 * ndp) == 0 and width == 2 * rows
+        if groups == lax.axis_size("psr") == 2 * 2 and tiled:
+            return fused(basis, *rest)
+        return on_device(basis, *rest)
+
     return jax.shard_map(
-        on_device,
+        step,
         mesh=mesh,
         in_specs=(
             P(("dp", "psr"), None, None, None, None),

time: 186 us -> 33.4 us (0.18)
  waiting for transfers between devices: 95.7 us -> 0 us
  blocking collectives: 44.1 us -> 0 us
  Pallas kernels: 0 us -> 28.5 us
  between operations: 16.7 us -> 0.64 us
  matrix products: 13.5 us -> 0 us
  other arithmetic: 12.3 us -> 0 us
    reduce_scatter x1 -> x0, waiting for transfers between devices: 95.7 us -> none  [on_device(): lax.psum_scatter(gram_rows, ('dp', 'psr'), scatter_dimension=0, tiled=True)]
    unnamed x1 -> x0, blocking collectives: 44.1 us -> none
    pallas_call x0 -> x1, Pallas kernels: none -> 28.5 us  [fused(): pl.pallas_call(functools.partial(kernel, ndp, norm_rows, all_rows), out_s...]
    dot_general x8 -> x0, matrix products: 13.5 us -> none  [the longest x4 9.01 us: slot_terms(): jnp.einsum('gslk,gslm->gkm', basis, masked, preferred_element_type=jnp.fl...]
    reduce_sum x5 -> x0, other arithmetic: 5.9 us -> none  [the longest x1 2.84 us: slot_terms(): project = jnp.sum(weighted.astype(jnp.float32) * res[..., None], axis=2)]
    unnamed x2 -> x3, local copies, waits for them, and re-layouts: 0.01 us -> 3.99 us
    div x3 -> x0, other arithmetic: 3.48 us -> none  [the longest x1 1.84 us: on_device(): totals = jnp.stack([summed[0], summed[1]]) / all_rows]
    another operation x5 -> x0, local copies, waits for them, and re-layouts: 2.56 us -> none  [slot_terms(): return (jnp.stack(grams, axis=1), jnp.stack(sums, axis=1), logdet, chi)]
  transfers between devices with their start and end apart: 1 -> 0, of which waited for: 1 -> 0; matrix products, arithmetic and copies ran while one was open for 2% -> 0% of each run, Pallas kernels for 0% -> 0%
where the time goes in v1:
time: 33.4 us; the launch traced here: 33.2 us
  Pallas kernels  28.5 us (85%)
  local copies, waits for them, and re-layouts  3.99 us (12%)
  between operations  0.64 us (2%)
    pallas_call x1, Pallas kernels, fused(): pl.pallas_call(functools.partial(kernel, ndp, norm_rows, all_rows), out_s...  28.5 us
    unnamed x3, local copies, waits for them, and re-layouts  3.99 us

profile of v1, /device:TPU:0, one launch (start us, length us, event | category | flops | bytes accessed | tf_op | source)
XLA Modules:
  0.0 33.2 jit_solution(10512179163199422447)
XLA Ops:
  0.6 28.5 %shard_map.85 = (f32[4,32,256]{2,1,0:T(8,128)}, f32[4,32]{1,0:T(4,128)}, f32[2]{0:T(128)}) custom-call(bf16[4,8,128,256]{3,2,1,0:T(8,128)(2,1)} %bitcast.6, bf16[4,8,128]{2,1,0:T(8,128)(2,1)} %bitcast.7, bf16[4,8,128]{2,1,0:T(8,128)(2,1)} %bitcast.8, s32[4,8]{1,0:T(4,128)} %bitcast.9, s32[4,8]{1,0:T(4,128)} %bitcast.10, f32[1,16]{1,0:T(1,128)} %bitcast.11), custom_call_target="tpu_custom_call" | custom-call | tf_op jit(solution)/shard_map/pallas_call | solution.py:280
  29.2 1.6 %copy.12 = f32[4,32,256]{2,1,0:T(8,128)} copy(f32[4,32,256]{2,1,0:T(8,128)} %get-tuple-element.6) | data formatting | bytes 262144
  30.7 1.3 %copy.13 = f32[4,32]{1,0:T(4,128)} copy(f32[4,32]{1,0:T(4,128)} %get-tuple-element.7) | data formatting | bytes 1024
  32.0 1.2 %copy.14 = f32[2]{0:T(128)} copy(f32[2]{0:T(128)} %get-tuple-element.8) | data formatting | bytes 16

commit v2 on v1

--- a/solution.py
+++ b/solution.py
@@ -98,17 +98,39 @@
     return gram, rhs, tot
 
 
+def triangle(n):
+    return lax.broadcasted_iota(jnp.int32, (n, n), 0), lax.broadcasted_iota(jnp.int32, (n, n), 1)
+
+
+def pack(full):
+    hw = full.shape[0] // 2
+    r, c = triangle(hw)
+    low = full[hw:, hw:]
+    diag = jnp.sum(jnp.where(r == c, low, F32(0.0)), axis=0, keepdims=True)
+    both = jnp.where(r <= c, full[:hw, :hw], low)
+    return jnp.concatenate([full[:hw, hw:], both, jnp.broadcast_to(diag, (16, hw))], axis=0)
+
+
+def unpack(packed):
+    hw = packed.shape[1]
+    r, c = triangle(hw)
+    cross, both = packed[:hw], packed[hw : 2 * hw]
+    diag = jnp.broadcast_to(packed[2 * hw : 2 * hw + 1], (hw, hw))
+    turned = both.T
+    top = jnp.concatenate([jnp.where(r <= c, both, turned), cross], axis=1)
+    low = jnp.where(r > c, both, jnp.where(r == c, diag, turned))
+    return jnp.concatenate([top, jnp.concatenate([cross.T, low], axis=1)], axis=0)
+
+
 def kernel(
-    ndp, norm_rows, all_rows,
-    basis_ref, res_ref, sig_ref, cnt_ref, pul_ref, ecorr_ref,
+    ndp,
+    basis_ref, res_in, sig_in, cnt_in, pul_in, ecorr_in,
     gram_ref, rhs_ref, tot_ref,
-    bbuf, out0, in0, out1, in1, own_a, own_b, send_a, send_b,
-    in_y, in_xa, in_xb, out_x, in_x, out_y, in_y2, part, out_z, in_z,
+    bbuf, res_ref, sig_ref, cnt_ref, pul_ref, ecorr_ref, out_c, in_c, out_y, in_y, whole, out_x, in_x, out_z, in_z,
     s_core, r_core, s_y, r_y, s_x, r_x, s_z, r_z,
-    load_sem, send_sem, recv_sem, zsend_sem, zrecv_sem,
+    load_sem, send_sem, recv_sem,
 ):
     nz = ndp // 2
-    half = PG // 2
     dp = lax.axis_index("dp")
     psr = lax.axis_index("psr")
     c, y = psr % 2, psr // 2
@@ -119,6 +141,12 @@
     x_peer = (z * 2 + x2, psr)
     order = (y2 * 2 + c2, y2 * 2 + c, y * 2 + c2, psr)
 
+    small_loads = []
+    pairs = ((sig_in, sig_ref), (cnt_in, cnt_ref), (res_in, res_ref), (pul_in, pul_ref))
+    for i, (src, dst) in enumerate(pairs + ((ecorr_in, ecorr_ref),)):
+        load = pltpu.make_async_copy(src, dst, load_sem.at[len(order) + i])
+        load.start()
+        small_loads.append(load)
     loads = []
     for i, g in enumerate(order):
         load = pltpu.make_async_copy(basis_ref.at[g], bbuf.at[i], load_sem.at[i])
@@ -130,138 +158,131 @@
     for peer in [core_peer, y_peer, x_peer] + z_peers:
         pl.semaphore_signal(barrier, inc=1, device_id=peer, device_id_type=MESH)
 
-    def send(i, src, dst, peer):
+    copies = []
+
+    def send(src, dst, peer):
+        i = len(copies)
         copy = pltpu.make_async_remote_copy(
             src_ref=src, dst_ref=dst, send_sem=send_sem.at[i], recv_sem=recv_sem.at[i],
             device_id=peer, device_id_type=MESH,
         )
         copy.start()
+        copies.append(copy)
         return copy
-
-    def shaped(v, ref):
-        return v.reshape(ref.shape[1:])
 
     def terms(i):
         loads[i].wait()
         return group_terms(order[i], bbuf.at[i], res_ref, sig_ref, cnt_ref, pul_ref, ecorr_ref)
 
-    gram, rhs0, tot = terms(0)
+    def core_send(n, value):
+        out_c[n] = value.astype(BF16)
+        return send(out_c.at[n], in_c.at[n], core_peer)
+
+    for load in small_loads:
+        load.wait()
+    gram0, rhs0, tot = terms(0)
+    first = pack(gram0(0))
+    pl.semaphore_wait(barrier, 2 + nz)
+    core = [core_send(0, first), core_send(1, pack(gram0(1)))]
+    gram1, rhs1, t = terms(1)
+    tot = tot + t
+    y_copies = []
     for m in range(PG):
-        out0[m] = shaped(gram(m).astype(BF16), out0)
-    pl.semaphore_wait(barrier, 2 + nz)
-    c0 = send(0, out0, in0, core_peer)
-
-    gram, rhs1, t = terms(1)
+        own = pack(gram1(m))
+        core[m].wait_recv()
+        out_y[m] = (own + in_c[m].astype(F32)).astype(BF16)
+        y_copies.append(send(out_y.at[m], in_y.at[m], y_peer))
+        if m + 2 < PG:
+            core.append(core_send(m + 2, pack(gram0(m + 2))))
+
+    gram2, rhs2, t = terms(2)
     tot = tot + t
     for m in range(PG):
-        own_a[m] = shaped(gram(m), own_a)
-
-    gram, rhs2, t = terms(2)
+        core.append(core_send(PG + m, pack(gram2(m))))
+    gram3, rhs3, t = terms(3)
     tot = tot + t
-    for m in range(PG):
-        out1[m] = shaped(gram(m).astype(BF16), out1)
-    c1 = send(1, out1, in1, core_peer)
-
-    c0.wait_recv()
-    send_a[...] = (own_a[...] + in0[...].astype(F32)).astype(BF16)
-    cy = send(2, send_a.at[pl.ds(0, half)], in_y, y_peer)
-    cxa = send(3, send_a.at[pl.ds(half, PG - half), :, x2], in_xa, x_peer)
-
-    gram, rhs3, t = terms(3)
-    tot = tot + t
-    for m in range(PG):
-        own_b[m] = shaped(gram(m), own_b)
-
     pad = jnp.zeros((3, tot.shape[1]), F32)
     s_core[...] = jnp.concatenate([rhs0, rhs2, tot, pad, jnp.zeros((4, tot.shape[1]), F32)], axis=0)
-    cs0 = send(4, s_core, r_core, core_peer)
-
-    c1.wait_recv()
-    own_b[...] = own_b[...] + in1[...].astype(F32)
-    send_b[...] = own_b[pl.ds(half, PG - half), :, x2].astype(BF16)
-    cxb = send(5, send_b, in_xb, x_peer)
-
-    cs0.wait_recv()
+    small_c = send(s_core, r_core, core_peer)
+
+    x_copies = []
+    z_copies = []
+
+    def to_x(m):
+        own = pack(gram3(m))
+        core[PG + m].wait_recv()
+        own = own + in_c[PG + m].astype(F32)
+        y_copies[m].wait_recv()
+        full = unpack(own + in_y[m].astype(F32)).reshape(whole.shape[1:])
+        whole[m] = full
+        out_x[m] = full.astype(BF16)
+        x_copies.append(send(out_x.at[m, :, x2], in_x.at[m], x_peer))
+
+    def to_z(m):
+        x_copies[m].wait_recv()
+        sent = []
+        for k in range(1, nz):
+            zt = (z + k) % nz
+            out_z[m, k - 1] = (whole[m, zt, x] + in_x[m, zt].astype(F32)).astype(BF16)
+            sent.append(send(out_z.at[m, k - 1], in_z.at[m, k - 1], z_peers[k - 1]))
+        z_copies.append(sent)
+
+    to_x(0)
+    small_c.wait_recv()
     rhs1 = rhs1 + r_core[0:PG]
     rhs3 = rhs3 + r_core[PG : 2 * PG]
     tot = tot + r_core[2 * PG : 2 * PG + 1]
     s_y[...] = jnp.concatenate([rhs1, tot, pad], axis=0)
-    cs1 = send(6, s_y, r_y, y_peer)
-
-    cxa.wait_recv()
-    out_y[...] = (
-        send_a[pl.ds(half, PG - half), :, x].astype(F32) + in_xa[...].astype(F32)
-    ).astype(BF16)
-    cy2 = send(7, out_y, in_y2, y_peer)
-
-    cy.wait_recv()
-    out_x[...] = (own_b[pl.ds(0, half), :, x2] + in_y[:, :, x2].astype(F32)).astype(BF16)
-    cx1 = send(8, out_x, in_x, x_peer)
-    part[0:half] = own_b[pl.ds(0, half), :, x] + in_y[:, :, x].astype(F32)
-
-    cs1.wait_recv()
+    small_y = send(s_y, r_y, y_peer)
+    to_x(1)
+    to_z(0)
+    to_x(2)
+    to_z(1)
+    small_y.wait_recv()
     rhs3 = rhs3 + r_y[0:PG]
     tot = tot + r_y[PG : PG + 1]
     s_x[...] = jnp.concatenate([rhs3, tot, pad], axis=0)
-    cs2 = send(9, s_x, r_x, x_peer)
-
-    def z_send(h, k, src, dst):
-        n = h * (nz - 1) + k - 1
-        copy = pltpu.make_async_remote_copy(
-            src_ref=src, dst_ref=dst, send_sem=zsend_sem.at[n], recv_sem=zrecv_sem.at[n],
-            device_id=z_peers[k - 1], device_id_type=MESH,
-        )
-        copy.start()
-        return copy
-
-    z_copies = []
-
-    def z_stage(h):
-        piece = pl.ds(h * half, half)
-        for k in range(1, nz):
-            zt = (z + k) % nz
-            out_z[piece, k - 1] = part[piece, zt].astype(BF16)
-            z_copies.append(z_send(h, k, out_z.at[piece, k - 1], in_z.at[piece, k - 1]))
-
-    cxb.wait_recv()
-    cy2.wait_recv()
-    part[half:PG] = (
-        own_b[pl.ds(half, PG - half), :, x] + in_xb[...].astype(F32) + in_y2[...].astype(F32)
-    )
-    z_stage(1)
-    cx1.wait_recv()
-    part[0:half] = part[0:half] + in_x[...].astype(F32)
-    z_stage(0)
-
-    cs2.wait_recv()
+    small_x = send(s_x, r_x, x_peer)
+    for m in range(3, PG):
+        to_x(m)
+        to_z(m - 1)
+    small_x.wait_recv()
     rhs3 = rhs3 + r_x[0:PG]
     tot = tot + r_x[PG : PG + 1]
     s_z[...] = jnp.concatenate([rhs3, tot, pad], axis=0)
-    small = [z_send(2, k, s_z, r_z.at[k - 1]) for k in range(1, nz)]
-
-    for h in (1, 0):
-        piece = pl.ds(h * half, half)
-        acc = part[piece, z]
+    small_z = [send(s_z, r_z.at[k - 1], z_peers[k - 1]) for k in range(1, nz)]
+    to_z(PG - 1)
+
+    def finish(m):
+        acc = whole[m, z, x] + in_x[m, z].astype(F32)
         for k in range(1, nz):
-            z_copies[(1 - h) * (nz - 1) + k - 1].wait_recv()
-            acc = acc + in_z[piece, k - 1].astype(F32)
-        gram_ref[piece] = acc / norm_rows
-
+            z_copies[m][k - 1].wait_recv()
+            acc = acc + in_z[m, k - 1].astype(F32)
+        gram_ref[m] = acc
+
+    for m in range(PG - 1):
+        finish(m)
     for k in range(1, nz):
-        small[k - 1].wait_recv()
+        small_z[k - 1].wait_recv()
         rhs3 = rhs3 + r_z[k - 1, 0:PG]
         tot = tot + r_z[k - 1, PG : PG + 1]
     share = rhs_ref.shape[1]
     mine = jnp.zeros((PG, share), F32)
     for e in range(ndp):
         mine = mine + jnp.where(dp == e, rhs3[:, e * share : (e + 1) * share], F32(0.0))
-    rhs_ref[...] = mine / norm_rows
-    rows = tot.shape[1] // 2
-    tot_ref[0] = jnp.sum(tot[:, :rows]) / all_rows
-    tot_ref[1] = jnp.sum(tot[:, rows:]) / all_rows
-
-    for copy in [c0, c1, cy, cxa, cs0, cxb, cs1, cy2, cx1, cs2] + z_copies + small:
+    rhs_ref[...] = mine
+    tot_ref[...] = tot
+    finish(PG - 1)
+    for copy in copies:
         copy.wait_send()
+
+
+def scale_kernel(norm_rows, all_rows, gram_in, rhs_in, tot_in, gram_ref, rhs_ref, tot_ref):
+    gram_ref[...] = gram_in[...] / norm_rows
+    rhs_ref[...] = rhs_in[...] / norm_rows
+    rows = tot_in.shape[1] // 2
+    tot_ref[0] = jnp.sum(tot_in[:, :rows]) / all_rows
+    tot_ref[1] = jnp.sum(tot_in[:, rows:]) / all_rows
 
 
 def fused(basis, residual, sigma, counts, pulsar, ecorr):
@@ -269,59 +290,59 @@
     groups, slots, rows, width = basis.shape[1:]
     share = width // ndp
     nz = ndp // 2
-    half = PG // 2
     norm_rows = float(ndp * slots * rows)
     all_rows = float(ndp * groups * groups * slots * rows)
     vmem = pl.BlockSpec(memory_space=pltpu.VMEM)
-    full = (PG, nz, 2, share, width)
-    hfull = (half, nz, 2, share, width)
-    hpar = (half, nz, share, width)
-    n_z = 3 * (nz - 1)
+    packed = (width + 16, width // 2)
+    n_copies = 4 * PG + (nz - 1) * (PG + 1) + 3
+    small = pltpu.VMEM((2 * PG, width), F32)
+    sums = pl.pallas_call(
+        functools.partial(kernel, ndp),
+        out_shape=(
+            jax.ShapeDtypeStruct((PG, share, width), F32),
+            jax.ShapeDtypeStruct((PG, share), F32),
+            jax.ShapeDtypeStruct((1, 2 * rows), F32),
+        ),
+        in_specs=[pl.BlockSpec(memory_space=pltpu.HBM)] * 6,
+        out_specs=(vmem, vmem, vmem),
+        scratch_shapes=[
+            pltpu.VMEM((groups, slots, rows, width), BF16),
+            pltpu.VMEM((groups, slots, rows), BF16),
+            pltpu.VMEM((groups, slots, rows), BF16),
+            pltpu.VMEM((groups, slots), jnp.int32),
+            pltpu.VMEM((groups, slots), jnp.int32),
+            pltpu.VMEM((1, ecorr.shape[0]), F32),
+            pltpu.VMEM((2 * PG,) + packed, BF16),
+            pltpu.VMEM((2 * PG,) + packed, BF16),
+            pltpu.VMEM((PG,) + packed, BF16),
+            pltpu.VMEM((PG,) + packed, BF16),
+            pltpu.VMEM((PG, nz, 2, share, width), F32),
+            pltpu.VMEM((PG, nz, 2, share, width), BF16),
+            pltpu.VMEM((PG, nz, share, width), BF16),
+            pltpu.VMEM((PG, nz - 1, share, width), BF16),
+            pltpu.VMEM((PG, nz - 1, share, width), BF16),
+            pltpu.VMEM((4 * PG, width), F32),
+            pltpu.VMEM((4 * PG, width), F32),
+            small, small, small, small, small,
+            pltpu.VMEM((nz - 1, 2 * PG, width), F32),
+            pltpu.SemaphoreType.DMA((groups + 5,)),
+            pltpu.SemaphoreType.DMA((n_copies,)),
+            pltpu.SemaphoreType.DMA((n_copies,)),
+        ],
+        compiler_params=pltpu.CompilerParams(
+            collective_id=0, has_side_effects=True
+        ),
+    )(basis[0], residual[0], sigma[0], counts[0], pulsar[0], ecorr.reshape(1, -1))
     return pl.pallas_call(
-        functools.partial(kernel, ndp, norm_rows, all_rows),
+        functools.partial(scale_kernel, norm_rows, all_rows),
         out_shape=(
             jax.ShapeDtypeStruct((PG, share, width), F32),
             jax.ShapeDtypeStruct((PG, share), F32),
             jax.ShapeDtypeStruct((2,), F32),
         ),
-        in_specs=[pl.BlockSpec(memory_space=pl.ANY)] + [vmem] * 5,
+        in_specs=[vmem] * 3,
         out_specs=(vmem, vmem, pl.BlockSpec(memory_space=pltpu.SMEM)),
-        scratch_shapes=[
-            pltpu.VMEM((groups, slots, rows, width), BF16),
-            pltpu.VMEM(full, BF16),
-            pltpu.VMEM(full, BF16),
-            pltpu.VMEM(full, BF16),
-            pltpu.VMEM(full, BF16),
-            pltpu.VMEM(full, F32),
-            pltpu.VMEM(full, F32),
-            pltpu.VMEM(full, BF16),
-            pltpu.VMEM(hpar, BF16),
-            pltpu.VMEM(hfull, BF16),
-            pltpu.VMEM(hpar, BF16),
-            pltpu.VMEM(hpar, BF16),
-            pltpu.VMEM(hpar, BF16),
-            pltpu.VMEM(hpar, BF16),
-            pltpu.VMEM(hpar, BF16),
-            pltpu.VMEM(hpar, BF16),
-            pltpu.VMEM((PG, nz, share, width), F32),
-            pltpu.VMEM((PG, nz - 1, share, width), BF16),
-            pltpu.VMEM((PG, nz - 1, share, width), BF16),
-            pltpu.VMEM((4 * PG, width), F32),
-            pltpu.VMEM((4 * PG, width), F32),
-            pltpu.VMEM((2 * PG, width), F32),
-            pltpu.VMEM((2 * PG, width), F32),
-            pltpu.VMEM((2 * PG, width), F32),
-            pltpu.VMEM((2 * PG, width), F32),
-            pltpu.VMEM((2 * PG, width), F32),
-            pltpu.VMEM((nz - 1, 2 * PG, width), F32),
-            pltpu.SemaphoreType.DMA((groups,)),
-            pltpu.SemaphoreType.DMA((10,)),
-            pltpu.SemaphoreType.DMA((10,)),
-            pltpu.SemaphoreType.DMA((n_z,)),
-            pltpu.SemaphoreType.DMA((n_z,)),
-        ],
-        compiler_params=pltpu.CompilerParams(collective_id=0, has_side_effects=True),
-    )(basis[0], residual[0], sigma[0], counts[0], pulsar[0], ecorr.reshape(1, -1))
+    )(*sums)
 
 
 def slot_terms(basis, residual, sigma, counts, pulsar, group_ids, ecorr):
@@ -396,7 +417,7 @@
     def step(basis, *rest):
         groups, _, rows, width = basis.shape[1:]
         ndp = lax.axis_size("dp")
-        tiled = ndp % 2 == 0 and ndp > 2 and width % (16 * ndp) == 0 and width == 2 * rows
+        tiled = ndp % 2 == 0 and ndp > 2 and width % (16 * ndp) == 0 and width % 256 == 0 and width == 2 * rows
         if groups == lax.axis_size("psr") == 2 * 2 and tiled:
             return fused(basis, *rest)
         return on_device(basis, *rest)

time: 33.4 us -> 28.1 us (0.84)
  local copies, waits for them, and re-layouts: 3.99 us -> 0 us
  Pallas kernels: 28.5 us -> 27.2 us
    unnamed x3 -> x0, local copies, waits for them, and re-layouts: 3.99 us -> none
    pallas_call x1 -> x2, Pallas kernels: 28.5 us -> 27.2 us  [the longest x1 25.6 us: fused(): pl.pallas_call(functools.partial(kernel, ndp), out_shape=(jax.ShapeDtypeS...]
where the time goes in v2:
time: 28.1 us; the launch traced here: 27.8 us
  Pallas kernels  27.2 us (97%)
  between operations  0.64 us (2%)
    pallas_call x1, Pallas kernels, fused(): pl.pallas_call(functools.partial(kernel, ndp), out_shape=(jax.ShapeDtypeS...  25.6 us
    pallas_call x1, Pallas kernels, fused(): pl.pallas_call(functools.partial(scale_kernel, norm_rows, all_rows), out_...  1.59 us

profile of v2, /device:TPU:0, one launch (start us, length us, event | category | flops | bytes accessed | tf_op | source)
XLA Modules:
  0.0 27.8 jit_solution(14516158685717882458)
XLA Ops:
  0.6 25.6 %shard_map.85 = (f32[4,32,256]{2,1,0:T(8,128)}, f32[4,32]{1,0:T(4,128)}, f32[1,256]{1,0:T(1,128)}) custom-call(bf16[4,8,128,256]{3,2,1,0:T(8,128)(2,1)} %bitcast.6, bf16[4,8,128]{2,1,0:T(8,128)(2,1)} %bitcast.7, bf16[4,8,128]{2,1,0:T(8,128)(2,1)} %bitcast.8, s32[4,8]{1,0:T(4,128)} %bitcast.9, s32[4,8]{1,0:T(4,128)} %bitcast.10, f32[1,16]{1,0:T(1,128)} %bitcast.11), custom_call_target="tpu_custom_call" | custom-call | tf_op jit(solution)/shard_map/pallas_call | solution.py:299
  26.2 1.6 %shard_map.86 = (f32[4,32,256]{2,1,0:T(8,128)}, f32[4,32]{1,0:T(4,128)}, f32[2]{0:T(128)}) custom-call(f32[4,32,256]{2,1,0:T(8,128)} %get-tuple-element.6.gram_in, f32[4,32]{1,0:T(4,128)} %get-tuple-element.7.rhs_in, f32[1,256]{1,0:T(1,128)} %get-tuple-element.8.tot_in), custom_call_target="tpu_custom_call" | custom-call | tf_op jit(solution)/shard_map/pallas_call | solution.py:336

commit v3 on v2

--- a/solution.py
+++ b/solution.py
@@ -197,33 +197,36 @@
 
     gram2, rhs2, t = terms(2)
     tot = tot + t
-    for m in range(PG):
-        core.append(core_send(PG + m, pack(gram2(m))))
     gram3, rhs3, t = terms(3)
     tot = tot + t
     pad = jnp.zeros((3, tot.shape[1]), F32)
     s_core[...] = jnp.concatenate([rhs0, rhs2, tot, pad, jnp.zeros((4, tot.shape[1]), F32)], axis=0)
     small_c = send(s_core, r_core, core_peer)
 
+    for m in range(2):
+        core.append(core_send(PG + m, pack(gram2(m))))
     x_copies = []
     z_copies = []
 
     def to_x(m):
         own = pack(gram3(m))
+        if m + 2 < PG:
+            core.append(core_send(PG + m + 2, pack(gram2(m + 2))))
         core[PG + m].wait_recv()
         own = own + in_c[PG + m].astype(F32)
         y_copies[m].wait_recv()
-        full = unpack(own + in_y[m].astype(F32)).reshape(whole.shape[1:])
-        whole[m] = full
-        out_x[m] = full.astype(BF16)
-        x_copies.append(send(out_x.at[m, :, x2], in_x.at[m], x_peer))
+        full = unpack(own + in_y[m].astype(F32))
+        full = full.reshape(nz, 2, *whole.shape[2:])
+        out_x[m] = jnp.where(x == 0, full[:, 1], full[:, 0]).astype(BF16)
+        x_copies.append(send(out_x.at[m], in_x.at[m], x_peer))
+        whole[m] = jnp.where(x == 0, full[:, 0], full[:, 1])
 
     def to_z(m):
         x_copies[m].wait_recv()
         sent = []
         for k in range(1, nz):
             zt = (z + k) % nz
-            out_z[m, k - 1] = (whole[m, zt, x] + in_x[m, zt].astype(F32)).astype(BF16)
+            out_z[m, k - 1] = (whole[m, zt] + in_x[m, zt].astype(F32)).astype(BF16)
             sent.append(send(out_z.at[m, k - 1], in_z.at[m, k - 1], z_peers[k - 1]))
         z_copies.append(sent)
 
@@ -254,7 +257,7 @@
     to_z(PG - 1)
 
     def finish(m):
-        acc = whole[m, z, x] + in_x[m, z].astype(F32)
+        acc = whole[m, z] + in_x[m, z].astype(F32)
         for k in range(1, nz):
             z_copies[m][k - 1].wait_recv()
             acc = acc + in_z[m, k - 1].astype(F32)
@@ -316,8 +319,8 @@
             pltpu.VMEM((2 * PG,) + packed, BF16),
             pltpu.VMEM((PG,) + packed, BF16),
             pltpu.VMEM((PG,) + packed, BF16),
-            pltpu.VMEM((PG, nz, 2, share, width), F32),
-            pltpu.VMEM((PG, nz, 2, share, width), BF16),
+            pltpu.VMEM((PG, nz, share, width), F32),
+            pltpu.VMEM((PG, nz, share, width), BF16),
             pltpu.VMEM((PG, nz, share, width), BF16),
             pltpu.VMEM((PG, nz - 1, share, width), BF16),
             pltpu.VMEM((PG, nz - 1, share, width), BF16),

time: 28.1 us -> 28.1 us (level)
  no operation moved by 1% of the time
where the time goes in v3:
time: 28.1 us; the launch traced here: 27.9 us
  Pallas kernels  27.2 us (97%)
  between operations  0.64 us (2%)
    pallas_call x1, Pallas kernels, fused(): pl.pallas_call(functools.partial(kernel, ndp), out_shape=(jax.ShapeDtypeS...  25.7 us
    pallas_call x1, Pallas kernels, fused(): pl.pallas_call(functools.partial(scale_kernel, norm_rows, all_rows), out_...  1.59 us

profile of v3, /device:TPU:0, one launch (start us, length us, event | category | flops | bytes accessed | tf_op | source)
XLA Modules:
  0.0 27.9 jit_solution(9385592704197712301)
XLA Ops:
  0.6 25.7 %shard_map.85 = (f32[4,32,256]{2,1,0:T(8,128)}, f32[4,32]{1,0:T(4,128)}, f32[1,256]{1,0:T(1,128)}) custom-call(bf16[4,8,128,256]{3,2,1,0:T(8,128)(2,1)} %bitcast.6, bf16[4,8,128]{2,1,0:T(8,128)(2,1)} %bitcast.7, bf16[4,8,128]{2,1,0:T(8,128)(2,1)} %bitcast.8, s32[4,8]{1,0:T(4,128)} %bitcast.9, s32[4,8]{1,0:T(4,128)} %bitcast.10, f32[1,16]{1,0:T(1,128)} %bitcast.11), custom_call_target="tpu_custom_call" | custom-call | tf_op jit(solution)/shard_map/pallas_call | solution.py:302
  26.3 1.6 %shard_map.86 = (f32[4,32,256]{2,1,0:T(8,128)}, f32[4,32]{1,0:T(4,128)}, f32[2]{0:T(128)}) custom-call(f32[4,32,256]{2,1,0:T(8,128)} %get-tuple-element.6.gram_in, f32[4,32]{1,0:T(4,128)} %get-tuple-element.7.rhs_in, f32[1,256]{1,0:T(1,128)} %get-tuple-element.8.tot_in), custom_call_target="tpu_custom_call" | custom-call | tf_op jit(solution)/shard_map/pallas_call | solution.py:339
